TPU v7x, 32 devices: a whole 2x2x4 slice. The times are simulated.
32 devices in a mesh: seg: 4 (over y, x), blk: 8 (over z, core).
Axes of the slice: x: 2, y: 2, z: 4, core: 2. Of those that a mesh axis runs over, the one named last changes fastest.
Arguments:
- state: float32 [32, 4, 16, 2304], P(('seg', 'blk')), may hold values from -6 to 6
- metric: float32 [32, 9, 16, 2304], P(('seg', 'blk')), may hold values from -0.4 to 3, as said below
- block_map: int32 [32], replicated, may hold values from 0 to 31, as said below
- links: int32 [32, 6, 4], replicated, may hold values from -1 to 31, as said below
Outputs:
- advanced: float32 [32, 4, 16, 2304], P(('seg', 'blk'))
Inputs may be any that keep to these rules, and one draw needn't show every extreme that they name: A permutation of the block numbers; device slot d = s * 8 + p (segment s, position p along its chain) holds block block_map[d]. `links`: entries are (partner block or -1, partner face, r_i, r_x). Face 0 of the block at position p > 0 joins face 1 of the block at position p - 1 of the same segment, face 1 at p < 7 joins face 0 at p + 1, both with zero flags; faces 0 at p = 0 and 1 at p = 7 have partner -1. A block has at most one of faces 2 to 5 with a partner, and some blocks have one; that partner lies at the same position p in another segment, names this block and face back with the same flags. Unused fields of a face with partner -1 are 0. `metric`: entries 0, 4 and 8 of the second dimension are positive.
All inputs are finite; a program needn't handle non-finite values.
Results may differ from a plain program's by a relative error of at most 0.0003.
Values sent between devices are 32-bit elements; how exact they have to be, the bound alone decides.
A program may use at most 64 MiB of HBM per device.

v0:
```python
import functools
import math

import jax
import jax.numpy as jnp
from jax import lax
from jax.experimental import pallas as pl
from jax.experimental.pallas import tpu as pltpu
from jax.sharding import PartitionSpec as P

time_step = 0.05
viscosity = 0.2
compress = 1.0
MESH = pl.DeviceIdType.MESH
LANES = 128
WALL = (-1.0, -1.0, -1.0, 1.0)


def split_index(index, size, count):
    quotient = jnp.zeros_like(index)
    for step in range(1, count):
        quotient += (index >= size * step).astype(jnp.int32)
    return quotient, index - size * quotient


def halves(value):
    lead = value.astype(jnp.bfloat16)
    return lead, (value - lead.astype(jnp.float32)).astype(jnp.bfloat16)


def select(flag, yes, no):
    return jnp.where(flag, yes, no)


def kernel(segs, chain, cross, state_hbm, metric_hbm, block_map, links, out_ref,
           first, second, geometry, total, pack_matrix, slope_matrix, bend_matrix,
           low_out, high_out, low_in, high_in, face_out, face_in,
           load_sem, chain_send, chain_recv, face_send, face_recv):
    length, width = out_ref.shape[1], out_ref.shape[2]
    chunk = math.lcm(cross, LANES)
    chunks = width // chunk
    inner = pl.ds(LANES, width)
    seg, pos = lax.axis_index("seg"), lax.axis_index("blk")
    me = seg * chain + pos
    has_before, has_after = pos > 0, pos < chain - 1
    before, after = lax.rem(pos + chain - 1, chain), lax.rem(pos + 1, chain)

    load_state = pltpu.make_async_copy(state_hbm.at[0], first.at[:, :, inner], load_sem.at[0])
    load_metric = pltpu.make_async_copy(metric_hbm.at[0], geometry, load_sem.at[1])
    load_state.start()
    load_metric.start()

    barrier = pltpu.get_barrier_semaphore()
    for offset in range(1, segs):
        pl.semaphore_signal(barrier, inc=1, device_id={"seg": lax.rem(seg + offset, segs)}, device_id_type=MESH)

    @pl.when(has_before)
    def _():
        pl.semaphore_signal(barrier, inc=1, device_id={"blk": before}, device_id_type=MESH)

    @pl.when(has_after)
    def _():
        pl.semaphore_signal(barrier, inc=1, device_id={"blk": after}, device_id_type=MESH)

    block = block_map[me]
    joins = [links[2 + side, 0, block] >= 0 for side in range(4)]
    partner, flip_along, flip_across = jnp.int32(-1), jnp.int32(0), jnp.int32(0)
    for side in range(4):
        partner = select(joins[side], links[2 + side, 0, block], partner)
        flip_along = select(joins[side], links[2 + side, 2, block], flip_along)
        flip_across = select(joins[side], links[2 + side, 3, block], flip_across)
    any_join = partner >= 0
    on_first = jnp.logical_or(joins[0], joins[1])
    on_high = jnp.logical_or(joins[1], joins[3])
    own_layers = [select(join, 0.0, 1.0) for join in joins]
    layer_stride = select(on_first, cross, 1)
    cell_stride = select(on_first, 1, cross)
    comes_from = []
    for offset in range(1, segs):
        device = lax.rem(seg + segs - offset, segs) * chain + pos
        comes_from.append(jnp.logical_and(any_join, block_map[device] == partner))

    pads = jnp.zeros((4, length, LANES), jnp.float32)
    for padded in (first, second):
        padded[:, :, :LANES] = pads
        padded[:, :, LANES + width:] = pads

    column = lax.broadcasted_iota(jnp.int32, (1, LANES), 1)
    layer, place = split_index(column, cross, 3)
    layer_place = select(on_high, cross - 1 - layer, layer)
    source = layer_place * layer_stride + place * cell_stride
    source = jnp.where(jnp.logical_and(layer < 2, any_join), source, -1)
    piece = 2 * LANES
    for part in range(width // piece):
        cells = lax.broadcasted_iota(jnp.int32, (piece, LANES), 0) + part * piece
        pack_matrix[part * piece:(part + 1) * piece, :] = (cells == source).astype(jnp.float32).astype(jnp.bfloat16)

    def pack(padded, turn):
        for c in range(4):
            for layer_index in range(2):
                row = 2 * c + layer_index
                low_out[turn, row:row + 1, :] = padded[c, layer_index:layer_index + 1, inner]
                high_out[turn, row:row + 1, :] = padded[c, length - 1 - layer_index:length - layer_index, inner]

    def pack_face(padded, turn):
        rows = 4 * length
        packed = jnp.zeros((2 * rows, LANES), jnp.float32)
        for part in range(width // piece):
            value = padded[:, :, LANES + part * piece:LANES + (part + 1) * piece].reshape(rows, piece)
            both = jnp.concatenate(halves(value), axis=0)
            packed += jnp.dot(both, pack_matrix[part * piece:(part + 1) * piece, :], preferred_element_type=jnp.float32)
        face_out[turn] = packed[:rows] + packed[rows:]

    def chain_copies(turn):
        to_before = pltpu.make_async_remote_copy(
            low_out.at[turn], high_in.at[turn], chain_send.at[turn, 0], chain_recv.at[turn, 0],
            device_id={"blk": before}, device_id_type=MESH)
        to_after = pltpu.make_async_remote_copy(
            high_out.at[turn], low_in.at[turn], chain_send.at[turn, 1], chain_recv.at[turn, 1],
            device_id={"blk": after}, device_id_type=MESH)
        return to_before, to_after

    def face_copies(turn):
        return [pltpu.make_async_remote_copy(
            face_out.at[turn], face_in.at[turn, offset - 1], face_send.at[turn, offset - 1],
            face_recv.at[turn, offset - 1], device_id={"seg": lax.rem(seg + offset, segs)}, device_id_type=MESH)
            for offset in range(1, segs)]

    def start_chain(turn):
        to_before, to_after = chain_copies(turn)

        @pl.when(has_before)
        def _():
            to_before.start()

        @pl.when(has_after)
        def _():
            to_after.start()

    def start_faces(turn):
        for copy in face_copies(turn):
            copy.start()

    def await_all(turn):
        to_before, to_after = chain_copies(turn)

        @pl.when(has_before)
        def _():
            to_before.wait_send()
            to_after.wait_recv()

        @pl.when(has_after)
        def _():
            to_after.wait_send()
            to_before.wait_recv()

        for copy in face_copies(turn):
            copy.wait()

    def build_spread():
        row = lax.broadcasted_iota(jnp.int32, (LANES, 1), 0)
        layer, place = split_index(row, cross, 3)
        place = select(flip_across == 1, cross - 1 - place, place)
        valid = jnp.logical_and(layer < 2, any_join)
        near = select(on_high, cross - 1, 0)
        spot = select(on_high, cross - 2 + layer, 1 - layer)
        outer = jnp.where(valid, spot * layer_stride + place * cell_stride, -1)
        edge = jnp.where(jnp.logical_and(valid, layer == 0), near * layer_stride + place * cell_stride, -1)
        sign = select(on_high, -1.0, 1.0)
        for part in range(width // LANES):
            cells = lax.broadcasted_iota(jnp.int32, (LANES, LANES), 1) + part * LANES
            is_outer = (cells == outer).astype(jnp.float32)
            is_edge = (cells == edge).astype(jnp.float32)
            slope = (sign * (is_outer - 8.0 * is_edge)).astype(jnp.bfloat16)
            bend = (16.0 * is_edge - is_outer).astype(jnp.bfloat16)
            at = slice(part * LANES, (part + 1) * LANES)
            slope_matrix[:LANES, at] = slope
            slope_matrix[LANES:, at] = slope
            bend_matrix[:LANES, at] = bend
            bend_matrix[LANES:, at] = bend

    lane = lax.broadcasted_iota(jnp.int32, (length, chunk), 1)
    row_of = lax.broadcasted_iota(jnp.int32, (length, chunk), 0)
    _, lane_k = split_index(lane, cross, chunk // cross)

    def central(value, minus2, minus1, plus1, plus2, bent):
        slope = (minus2 - plus2) + 8.0 * (plus1 - minus1)
        if not bent:
            return slope, None
        return slope, 16.0 * (minus1 + plus1) - (minus2 + plus2) - 30.0 * value

    def along(value, bent):
        def moved(step):
            rolled = pltpu.roll(value, step % length, 0)
            inside = row_of >= step if step > 0 else row_of < length + step
            return jnp.where(inside, rolled, 0.0)
        return central(value, moved(2), moved(1), moved(-1), moved(-2), bent)

    def across(wide, value, stride, index, low_factor, high_factor, bent):
        def moved(step):
            if step > 0:
                return pltpu.roll(wide[:, :LANES + chunk], step, 1)[:, LANES:]
            span = LANES + chunk
            return pltpu.roll(wide[:, LANES:], span + step, 1)[:, :chunk]
        minus2, minus1, plus1, plus2 = moved(2 * stride), moved(stride), moved(-stride), moved(-2 * stride)
        at0, at1, at_last1, at_last = index
        m1 = jnp.where(at0, low_factor * value, minus1)
        p1 = jnp.where(at_last, high_factor * value, plus1)
        m2 = jnp.where(at0, low_factor * plus1, jnp.where(at1, low_factor * minus1, minus2))
        p2 = jnp.where(at_last, high_factor * minus1, jnp.where(at_last1, high_factor * plus1, plus2))
        return central(value, m2, m1, p1, p2, bent)

    def weights(metric, values):
        carried = metric[0] * values[0] + metric[1] * values[1] + metric[2] * values[2]
        norm = viscosity * (metric[0] * metric[0] + metric[1] * metric[1] + metric[2] * metric[2])
        return carried, norm

    def rates_of(metric, values, slopes, bends):
        carried, norm = weights(metric, values)
        parts = [norm * bends[c] - carried * slopes[c] - metric[c] * slopes[3] for c in range(3)]
        parts.append(-compress * (metric[0] * slopes[0] + metric[1] * slopes[1] + metric[2] * slopes[2]))
        return parts

    def inside_rates(padded):
        def body(step, carry):
            start = pl.multiple_of(step * chunk, LANES)
            cell = lane + step * chunk
            k_at = (lane_k == 0, lane_k == 1, lane_k == cross - 2, lane_k == cross - 1)
            j_at = (cell < cross, jnp.logical_and(cell >= cross, cell < 2 * cross),
                    jnp.logical_and(cell >= width - 2 * cross, cell < width - cross), cell >= width - cross)
            wide = [padded[c, :, pl.ds(start, chunk + 2 * LANES)] for c in range(4)]
            values = [w[:, LANES:LANES + chunk] for w in wide]
            sums = None
            for direction in range(3):
                metric = [geometry[3 * direction + b, :, pl.ds(start, chunk)] for b in range(3)]
                slopes, bends = [], []
                for c in range(4):
                    if direction == 0:
                        slope, bend = along(values[c], c < 3)
                    else:
                        stride, at = ((cross, j_at), (1, k_at))[direction - 1]
                        low = WALL[c] * own_layers[2 * direction - 2]
                        high = WALL[c] * own_layers[2 * direction - 1]
                        slope, bend = across(wide[c], values[c], stride, at, low, high, c < 3)
                    slopes.append(slope)
                    bends.append(bend)
                parts = rates_of(metric, values, slopes, bends)
                sums = parts if sums is None else [a + b for a, b in zip(sums, parts)]
            for c in range(4):
                total[c, :, pl.ds(start, chunk)] = sums[c]
            return carry

        lax.fori_loop(0, chunks, body, 0)

    def outside_rates(padded, turn, finish):
        received = jnp.zeros((4 * length, LANES), jnp.float32)
        for index, here in enumerate(comes_from):
            received = jnp.where(here, face_in[turn, index], received)
        both = jnp.concatenate(halves(received), axis=1)
        target = lax.broadcasted_iota(jnp.int32, (4 * length, 1), 0)
        component, along_index = split_index(target, length, 4)
        along_index = select(flip_along == 1, length - 1 - along_index, along_index)
        target = component * length + along_index
        swap = (lax.broadcasted_iota(jnp.int32, (4 * length, 4 * length), 1) == target)
        swap = swap.astype(jnp.float32).astype(jnp.bfloat16)
        both = jnp.dot(swap, both, preferred_element_type=jnp.float32).astype(jnp.bfloat16)

        def body(step, carry):
            start = pl.multiple_of(step * chunk, LANES)
            at = pl.ds(start, chunk)
            values = [padded[c, :, pl.ds(pl.multiple_of(start + LANES, LANES), chunk)] for c in range(4)]
            metric = [geometry[b, :, at] for b in range(3)]
            low_own, high_own = low_out[turn, :, at], high_out[turn, :, at]
            low_got, high_got = low_in[turn, :, at], high_in[turn, :, at]
            slopes, bends = [], []
            for c in range(4):
                ghosts = []
                for got, own, there in ((low_got, low_own, has_before), (high_got, high_own, has_after)):
                    for layer_index in range(2):
                        row = 2 * c + layer_index
                        ghosts.append(jnp.where(there, got[row:row + 1], -WALL[c] * own[row:row + 1]))
                low0, low1, high0, high1 = ghosts
                slope = jnp.where(row_of == 0, low1 - 8.0 * low0, 0.0)
                slope = jnp.where(row_of == 1, low0, slope)
                slope = jnp.where(row_of == length - 2, -high0, slope)
                slopes.append(jnp.where(row_of == length - 1, 8.0 * high0 - high1, slope))
                if c < 3:
                    bend = jnp.where(row_of == 0, 16.0 * low0 - low1, 0.0)
                    bend = jnp.where(row_of == 1, -low0, bend)
                    bend = jnp.where(row_of == length - 2, -high0, bend)
                    bends.append(jnp.where(row_of == length - 1, 16.0 * high0 - high1, bend))
            sums = rates_of(metric, values, slopes, bends)
            metric = [jnp.where(on_first, geometry[3 + b, :, at], geometry[6 + b, :, at]) for b in range(3)]
            slope = jnp.dot(both, slope_matrix[:, at], preferred_element_type=jnp.float32)
            bend = jnp.dot(both[:3 * length], bend_matrix[:, at], preferred_element_type=jnp.float32)
            slopes = [slope[c * length:(c + 1) * length] for c in range(4)]
            bends = [bend[c * length:(c + 1) * length] for c in range(3)]
            parts = rates_of(metric, values, slopes, bends)
            for c in range(4):
                finish(c, start, values[c], total[c, :, at] + sums[c] + parts[c])
            return carry

        lax.fori_loop(0, chunks, body, 0)

    def finish_first(c, start, value, rate):
        second[c, :, pl.ds(pl.multiple_of(start + LANES, LANES), chunk)] = value + (time_step / 12.0) * rate

    def finish_second(c, start, value, rate):
        base = first[c, :, pl.ds(pl.multiple_of(start + LANES, LANES), chunk)]
        out_ref[c, :, pl.ds(start, chunk)] = 0.5 * base + 0.5 * (value + (time_step / 12.0) * rate)

    load_state.wait()
    pack(first, 0)
    pl.semaphore_wait(barrier, segs - 1 + has_before.astype(jnp.int32) + has_after.astype(jnp.int32))

    start_chain(0)
    pack_face(first, 0)
    start_faces(0)
    build_spread()
    load_metric.wait()
    inside_rates(first)
    await_all(0)
    outside_rates(first, 0, finish_first)

    pack(second, 1)
    start_chain(1)
    pack_face(second, 1)
    start_faces(1)
    inside_rates(second)
    await_all(1)
    outside_rates(second, 1, finish_second)


def on_device(state, metric, block_map, links):
    segs, chain = lax.axis_size("seg"), lax.axis_size("blk")
    _, parts, length, width = state.shape
    cross = math.isqrt(width)
    f32, bf16, dma = jnp.float32, jnp.bfloat16, pltpu.SemaphoreType.DMA
    result = pl.pallas_call(
        functools.partial(kernel, segs, chain, cross),
        out_shape=jax.ShapeDtypeStruct((parts, length, width), f32),
        in_specs=[pl.BlockSpec(memory_space=pl.ANY)] * 2 + [pl.BlockSpec(memory_space=pltpu.SMEM)] * 2,
        out_specs=pl.BlockSpec(memory_space=pltpu.VMEM),
        scratch_shapes=[
            pltpu.VMEM((parts, length, width + 2 * LANES), f32),
            pltpu.VMEM((parts, length, width + 2 * LANES), f32),
            pltpu.VMEM((9, length, width), f32),
            pltpu.VMEM((parts, length, width), f32),
            pltpu.VMEM((width, LANES), bf16),
            pltpu.VMEM((2 * LANES, width), bf16),
            pltpu.VMEM((2 * LANES, width), bf16),
            pltpu.VMEM((2, 2 * parts, width), f32),
            pltpu.VMEM((2, 2 * parts, width), f32),
            pltpu.VMEM((2, 2 * parts, width), f32),
            pltpu.VMEM((2, 2 * parts, width), f32),
            pltpu.VMEM((2, parts * length, LANES), f32),
            pltpu.VMEM((2, segs - 1, parts * length, LANES), f32),
            dma((2,)), dma((2, 2)), dma((2, 2)), dma((2, segs - 1)), dma((2, segs - 1)),
        ],
        compiler_params=pltpu.CompilerParams(collective_id=0, has_side_effects=True),
    )(state, metric, block_map, links.transpose(1, 2, 0))
    return result.reshape(state.shape)


def solution(mesh):
    in_specs = (P(("seg", "blk"), None, None, None), P(("seg", "blk"), None, None, None), P(), P())
    out_specs = P(("seg", "blk"), None, None, None)
    return jax.shard_map(
        on_device, mesh=mesh, in_specs=in_specs, out_specs=out_specs, check_vma=False
    )
```

profile of v0, /device:TPU:0, one launch (start us, length us, event | category | flops | bytes accessed | tf_op | source)
XLA Modules:
  0.0 18.2 jit_solution(14137292455079025513)
XLA Ops:
  0.0 16.3 %shard_map.46 = f32[4,16,2304]{2,1,0:T(8,128)} custom-call(f32[1,4,16,2304]{3,2,1,0:T(8,128)} %state_hbm.1, f32[1,9,16,2304]{3,2,1,0:T(8,128)} %metric_hbm.1, s32[32]{0:T(128)} %block_map.1, s32[6,4,32]{2,1,0:T(4,128)} %bitcast.3), custom_call_target="tpu_custom_call" | custom-call | tf_op jit(solution)/shard_map/pallas_call | solution.py:339
  16.3 1.9 %copy.6 = f32[1,4,16,2304]{3,2,1,0:T(8,128)} copy(f32[1,4,16,2304]{3,2,1,0:T(8,128)} %bitcast.2) | data formatting | bytes 1179648
where the time goes:
time: 18.4 us; the launch traced here: 18.2 us
  Pallas kernels  16.3 us (89%)
  local copies, waits for them, and re-layouts  1.92 us (10%)
    pallas_call x1, Pallas kernels, on_device(): pl.pallas_call(functools.partial(kernel, segs, chain, cross), out_shape=j...  16.3 us
    unnamed x1, local copies, waits for them, and re-layouts  1.92 us

commit v1 on v0

--- a/solution.py
+++ b/solution.py
@@ -34,6 +34,7 @@
 
 def kernel(segs, chain, cross, state_hbm, metric_hbm, block_map, links, out_ref,
            first, second, geometry, total, pack_matrix, slope_matrix, bend_matrix,
+           split, k_slope_uvw, k_slope_p, k_bend, slope_k, bend_k,
            low_out, high_out, low_in, high_in, face_out, face_in,
            load_sem, chain_send, chain_recv, face_send, face_recv):
     length, width = out_ref.shape[1], out_ref.shape[2]
@@ -104,12 +105,61 @@
 
     def pack_face(padded, turn):
         rows = 4 * length
-        packed = jnp.zeros((2 * rows, LANES), jnp.float32)
-        for part in range(width // piece):
-            value = padded[:, :, LANES + part * piece:LANES + (part + 1) * piece].reshape(rows, piece)
-            both = jnp.concatenate(halves(value), axis=0)
-            packed += jnp.dot(both, pack_matrix[part * piece:(part + 1) * piece, :], preferred_element_type=jnp.float32)
+        lead, trail = halves(padded[:, :, inner].reshape(rows, width))
+        split[0] = lead
+        split[1] = trail
+        both = jnp.concatenate([lead, trail], axis=0)
+        packed = jnp.dot(both, pack_matrix[...], preferred_element_type=jnp.float32)
         face_out[turn] = packed[:rows] + packed[rows:]
+
+    def build_k():
+        for matrix in (k_slope_uvw, k_slope_p, k_bend):
+            matrix[...] = jnp.zeros((2 * chunk, chunk), jnp.bfloat16)
+        low, high = own_layers[2], own_layers[3]
+        here = lax.broadcasted_iota(jnp.int32, (cross, LANES), 0)
+        column = lax.broadcasted_iota(jnp.int32, (cross, LANES), 1)
+        for group in range(chunk // cross):
+            first_row = group * cross
+            for tile in range(first_row // LANES, (first_row + cross - 1) // LANES + 1):
+                there = column + (tile * LANES - first_row)
+                there = jnp.where(jnp.logical_and(there >= 0, there < cross), there, 4 * width)
+                offset, mirrored = here - there, here + there
+
+                def at(index, value, factor):
+                    return jnp.where(index == value, factor, 0.0)
+
+                slope = at(offset, -2, 1.0) + at(offset, -1, -8.0) + at(offset, 1, 8.0) + at(offset, 2, -1.0)
+                bend = (at(offset, -2, -1.0) + at(offset, -1, 16.0) + at(offset, 0, -30.0)
+                        + at(offset, 1, 16.0) + at(offset, 2, -1.0))
+                end = 2 * cross - 2
+                wall_slope = (at(mirrored, 0, -8.0 * low) + at(mirrored, 1, low)
+                              + at(mirrored, end, 8.0 * high) + at(mirrored, end - 1, -high))
+                wall_bend = (at(mirrored, 0, 16.0 * low) + at(mirrored, 1, -low)
+                             + at(mirrored, end, 16.0 * high) + at(mirrored, end - 1, -high))
+                lanes = slice(tile * LANES, (tile + 1) * LANES)
+                for matrix, value in ((k_slope_uvw, slope + WALL[0] * wall_slope),
+                                      (k_slope_p, slope + WALL[3] * wall_slope),
+                                      (k_bend, bend + WALL[0] * wall_bend)):
+                    value = value.astype(jnp.bfloat16)
+                    matrix[first_row:first_row + cross, lanes] = value
+                    matrix[chunk + first_row:chunk + first_row + cross, lanes] = value
+
+    def along_k():
+        rows = 3 * length
+        parts = []
+        for step in range(chunks):
+            at = slice(step * chunk, (step + 1) * chunk)
+            parts.append(jnp.concatenate([split[0, :, at], split[1, :, at]], axis=1))
+        velocity = jnp.concatenate([part[:rows] for part in parts], axis=0)
+        pressure = jnp.concatenate([part[rows:] for part in parts], axis=0)
+        slope = jnp.dot(velocity, k_slope_uvw[...], preferred_element_type=jnp.float32)
+        bend = jnp.dot(velocity, k_bend[...], preferred_element_type=jnp.float32)
+        slope_p = jnp.dot(pressure, k_slope_p[...], preferred_element_type=jnp.float32)
+        for step in range(chunks):
+            at = slice(step * chunk, (step + 1) * chunk)
+            slope_k[:3, :, at] = slope[step * rows:(step + 1) * rows].reshape(3, length, chunk)
+            bend_k[:, :, at] = bend[step * rows:(step + 1) * rows].reshape(3, length, chunk)
+            slope_k[3, :, at] = slope_p[step * length:(step + 1) * length]
 
     def chain_copies(turn):
         to_before = pltpu.make_async_remote_copy(
@@ -181,7 +231,6 @@
 
     lane = lax.broadcasted_iota(jnp.int32, (length, chunk), 1)
     row_of = lax.broadcasted_iota(jnp.int32, (length, chunk), 0)
-    _, lane_k = split_index(lane, cross, chunk // cross)
 
     def central(value, minus2, minus1, plus1, plus2, bent):
         slope = (minus2 - plus2) + 8.0 * (plus1 - minus1)
@@ -196,18 +245,20 @@
             return jnp.where(inside, rolled, 0.0)
         return central(value, moved(2), moved(1), moved(-1), moved(-2), bent)
 
-    def across(wide, value, stride, index, low_factor, high_factor, bent):
+    def along_j(wide, value, low_factor, high_factor, bent):
         def moved(step):
             if step > 0:
                 return pltpu.roll(wide[:, :LANES + chunk], step, 1)[:, LANES:]
-            span = LANES + chunk
-            return pltpu.roll(wide[:, LANES:], span + step, 1)[:, :chunk]
-        minus2, minus1, plus1, plus2 = moved(2 * stride), moved(stride), moved(-stride), moved(-2 * stride)
-        at0, at1, at_last1, at_last = index
-        m1 = jnp.where(at0, low_factor * value, minus1)
-        p1 = jnp.where(at_last, high_factor * value, plus1)
-        m2 = jnp.where(at0, low_factor * plus1, jnp.where(at1, low_factor * minus1, minus2))
-        p2 = jnp.where(at_last, high_factor * minus1, jnp.where(at_last1, high_factor * plus1, plus2))
+            return pltpu.roll(wide[:, LANES:], LANES + chunk + step, 1)[:, :chunk]
+        minus2, minus1, plus1, plus2 = moved(2 * cross), moved(cross), moved(-cross), moved(-2 * cross)
+        m1, m2, p1, p2 = minus1, minus2, plus1, plus2
+        if low_factor is not None:
+            m1 = jnp.where(lane < cross, low_factor * value, minus1)
+            m2 = jnp.where(lane < cross, low_factor * plus1, jnp.where(lane < 2 * cross, low_factor * minus1, minus2))
+        if high_factor is not None:
+            p1 = jnp.where(lane >= chunk - cross, high_factor * value, plus1)
+            p2 = jnp.where(lane >= chunk - cross, high_factor * minus1,
+                           jnp.where(lane >= chunk - 2 * cross, high_factor * plus1, plus2))
         return central(value, m2, m1, p1, p2, bent)
 
     def weights(metric, values):
@@ -222,35 +273,39 @@
         return parts
 
     def inside_rates(padded):
-        def body(step, carry):
-            start = pl.multiple_of(step * chunk, LANES)
-            cell = lane + step * chunk
-            k_at = (lane_k == 0, lane_k == 1, lane_k == cross - 2, lane_k == cross - 1)
-            j_at = (cell < cross, jnp.logical_and(cell >= cross, cell < 2 * cross),
-                    jnp.logical_and(cell >= width - 2 * cross, cell < width - cross), cell >= width - cross)
+        def at_chunk(start, is_first, is_last):
+            at = pl.ds(start, chunk)
             wide = [padded[c, :, pl.ds(start, chunk + 2 * LANES)] for c in range(4)]
             values = [w[:, LANES:LANES + chunk] for w in wide]
             sums = None
             for direction in range(3):
-                metric = [geometry[3 * direction + b, :, pl.ds(start, chunk)] for b in range(3)]
-                slopes, bends = [], []
-                for c in range(4):
-                    if direction == 0:
-                        slope, bend = along(values[c], c < 3)
-                    else:
-                        stride, at = ((cross, j_at), (1, k_at))[direction - 1]
-                        low = WALL[c] * own_layers[2 * direction - 2]
-                        high = WALL[c] * own_layers[2 * direction - 1]
-                        slope, bend = across(wide[c], values[c], stride, at, low, high, c < 3)
-                    slopes.append(slope)
-                    bends.append(bend)
+                metric = [geometry[3 * direction + b, :, at] for b in range(3)]
+                if direction == 2:
+                    slopes = [slope_k[c, :, at] for c in range(4)]
+                    bends = [bend_k[c, :, at] for c in range(3)]
+                else:
+                    slopes, bends = [], []
+                    for c in range(4):
+                        if direction == 0:
+                            slope, bend = along(values[c], c < 3)
+                        else:
+                            low = WALL[c] * own_layers[0] if is_first else None
+                            high = WALL[c] * own_layers[1] if is_last else None
+                            slope, bend = along_j(wide[c], values[c], low, high, c < 3)
+                        slopes.append(slope)
+                        bends.append(bend)
                 parts = rates_of(metric, values, slopes, bends)
                 sums = parts if sums is None else [a + b for a, b in zip(sums, parts)]
             for c in range(4):
-                total[c, :, pl.ds(start, chunk)] = sums[c]
-            return carry
-
-        lax.fori_loop(0, chunks, body, 0)
+                total[c, :, at] = sums[c]
+
+        at_chunk(0, True, chunks == 1)
+        if chunks > 2:
+            @pl.loop(1, chunks - 1)
+            def _(step):
+                at_chunk(pl.multiple_of(step * chunk, LANES), False, False)
+        if chunks > 1:
+            at_chunk((chunks - 1) * chunk, False, True)
 
     def outside_rates(padded, turn, finish):
         received = jnp.zeros((4 * length, LANES), jnp.float32)
@@ -317,6 +372,8 @@
     pack_face(first, 0)
     start_faces(0)
     build_spread()
+    build_k()
+    along_k()
     load_metric.wait()
     inside_rates(first)
     await_all(0)
@@ -326,6 +383,7 @@
     start_chain(1)
     pack_face(second, 1)
     start_faces(1)
+    along_k()
     inside_rates(second)
     await_all(1)
     outside_rates(second, 1, finish_second)
@@ -335,10 +393,11 @@
     segs, chain = lax.axis_size("seg"), lax.axis_size("blk")
     _, parts, length, width = state.shape
     cross = math.isqrt(width)
+    chunk = math.lcm(cross, LANES)
     f32, bf16, dma = jnp.float32, jnp.bfloat16, pltpu.SemaphoreType.DMA
     result = pl.pallas_call(
         functools.partial(kernel, segs, chain, cross),
-        out_shape=jax.ShapeDtypeStruct((parts, length, width), f32),
+        out_shape=pltpu.VMEM((parts, length, width), f32),
         in_specs=[pl.BlockSpec(memory_space=pl.ANY)] * 2 + [pl.BlockSpec(memory_space=pltpu.SMEM)] * 2,
         out_specs=pl.BlockSpec(memory_space=pltpu.VMEM),
         scratch_shapes=[
@@ -349,6 +408,12 @@
             pltpu.VMEM((width, LANES), bf16),
             pltpu.VMEM((2 * LANES, width), bf16),
             pltpu.VMEM((2 * LANES, width), bf16),
+            pltpu.VMEM((2, parts * length, width), bf16),
+            pltpu.VMEM((2 * chunk, chunk), bf16),
+            pltpu.VMEM((2 * chunk, chunk), bf16),
+            pltpu.VMEM((2 * chunk, chunk), bf16),
+            pltpu.VMEM((parts, length, width), f32),
+            pltpu.VMEM((parts - 1, length, width), f32),
             pltpu.VMEM((2, 2 * parts, width), f32),
             pltpu.VMEM((2, 2 * parts, width), f32),
             pltpu.VMEM((2, 2 * parts, width), f32),

time: 18.4 us -> 16.6 us (0.902)
  local copies, waits for them, and re-layouts: 1.92 us -> 0.82 us
  Pallas kernels: 16.3 us -> 15.5 us
    unnamed x1, local copies, waits for them, and re-layouts: 1.92 us -> 0.82 us
    pallas_call x1, Pallas kernels: 16.3 us -> 15.5 us  [on_device(): pl.pallas_call(functools.partial(kernel, segs, chain, cross), out_shape=p...]
where the time goes in v1:
time: 16.6 us; the launch traced here: 16.3 us
  Pallas kernels  15.5 us (93%)
  local copies, waits for them, and re-layouts  0.82 us (5%)
    pallas_call x1, Pallas kernels, on_device(): pl.pallas_call(functools.partial(kernel, segs, chain, cross), out_shape=p...  15.5 us
    unnamed x1, local copies, waits for them, and re-layouts  0.82 us

profile of v1, /device:TPU:0, one launch (start us, length us, event | category | flops | bytes accessed | tf_op | source)
XLA Modules:
  0.0 16.3 jit_solution(3338614410500220225)
XLA Ops:
  0.0 15.5 %shard_map.46 = f32[4,16,2304]{2,1,0:T(8,128)S(1)} custom-call(f32[1,4,16,2304]{3,2,1,0:T(8,128)} %state_hbm.1, f32[1,9,16,2304]{3,2,1,0:T(8,128)} %metric_hbm.1, s32[32]{0:T(128)} %block_map.1, s32[6,4,32]{2,1,0:T(4,128)} %bitcast.3), custom_call_target="tpu_custom_call" | custom-call | tf_op jit(solution)/shard_map/pallas_call | solution.py:398
  15.5 0.8 %copy.6 = f32[1,4,16,2304]{3,2,1,0:T(8,128)} copy(f32[1,4,16,2304]{3,2,1,0:T(8,128)S(1)} %bitcast.2) | data formatting | bytes 1179648

commit v2 on v1

--- a/solution.py
+++ b/solution.py
@@ -191,7 +191,7 @@
         for copy in face_copies(turn):
             copy.start()
 
-    def await_all(turn):
+    def await_chain(turn):
         to_before, to_after = chain_copies(turn)
 
         @pl.when(has_before)
@@ -204,6 +204,7 @@
             to_after.wait_send()
             to_before.wait_recv()
 
+    def await_faces(turn):
         for copy in face_copies(turn):
             copy.wait()
 
@@ -307,19 +308,7 @@
         if chunks > 1:
             at_chunk((chunks - 1) * chunk, False, True)
 
-    def outside_rates(padded, turn, finish):
-        received = jnp.zeros((4 * length, LANES), jnp.float32)
-        for index, here in enumerate(comes_from):
-            received = jnp.where(here, face_in[turn, index], received)
-        both = jnp.concatenate(halves(received), axis=1)
-        target = lax.broadcasted_iota(jnp.int32, (4 * length, 1), 0)
-        component, along_index = split_index(target, length, 4)
-        along_index = select(flip_along == 1, length - 1 - along_index, along_index)
-        target = component * length + along_index
-        swap = (lax.broadcasted_iota(jnp.int32, (4 * length, 4 * length), 1) == target)
-        swap = swap.astype(jnp.float32).astype(jnp.bfloat16)
-        both = jnp.dot(swap, both, preferred_element_type=jnp.float32).astype(jnp.bfloat16)
-
+    def chain_rates(padded, turn):
         def body(step, carry):
             start = pl.multiple_of(step * chunk, LANES)
             at = pl.ds(start, chunk)
@@ -345,6 +334,29 @@
                     bend = jnp.where(row_of == length - 2, -high0, bend)
                     bends.append(jnp.where(row_of == length - 1, 16.0 * high0 - high1, bend))
             sums = rates_of(metric, values, slopes, bends)
+            for c in range(4):
+                total[c, :, at] += sums[c]
+            return carry
+
+        lax.fori_loop(0, chunks, body, 0)
+
+    def face_rates(padded, turn, finish):
+        received = jnp.zeros((4 * length, LANES), jnp.float32)
+        for index, here in enumerate(comes_from):
+            received = jnp.where(here, face_in[turn, index], received)
+        both = jnp.concatenate(halves(received), axis=1)
+        target = lax.broadcasted_iota(jnp.int32, (4 * length, 1), 0)
+        component, along_index = split_index(target, length, 4)
+        along_index = select(flip_along == 1, length - 1 - along_index, along_index)
+        target = component * length + along_index
+        swap = (lax.broadcasted_iota(jnp.int32, (4 * length, 4 * length), 1) == target)
+        swap = swap.astype(jnp.float32).astype(jnp.bfloat16)
+        both = jnp.dot(swap, both, preferred_element_type=jnp.float32).astype(jnp.bfloat16)
+
+        def body(step, carry):
+            start = pl.multiple_of(step * chunk, LANES)
+            at = pl.ds(start, chunk)
+            values = [padded[c, :, pl.ds(pl.multiple_of(start + LANES, LANES), chunk)] for c in range(4)]
             metric = [jnp.where(on_first, geometry[3 + b, :, at], geometry[6 + b, :, at]) for b in range(3)]
             slope = jnp.dot(both, slope_matrix[:, at], preferred_element_type=jnp.float32)
             bend = jnp.dot(both[:3 * length], bend_matrix[:, at], preferred_element_type=jnp.float32)
@@ -352,7 +364,7 @@
             bends = [bend[c * length:(c + 1) * length] for c in range(3)]
             parts = rates_of(metric, values, slopes, bends)
             for c in range(4):
-                finish(c, start, values[c], total[c, :, at] + sums[c] + parts[c])
+                finish(c, start, values[c], total[c, :, at] + parts[c])
             return carry
 
         lax.fori_loop(0, chunks, body, 0)
@@ -365,28 +377,32 @@
         out_ref[c, :, pl.ds(start, chunk)] = 0.5 * base + 0.5 * (value + (time_step / 12.0) * rate)
 
     load_state.wait()
+    pack_face(first, 0)
+    pl.semaphore_wait(barrier, segs - 1 + has_before.astype(jnp.int32) + has_after.astype(jnp.int32))
+
+    start_faces(0)
     pack(first, 0)
-    pl.semaphore_wait(barrier, segs - 1 + has_before.astype(jnp.int32) + has_after.astype(jnp.int32))
-
     start_chain(0)
-    pack_face(first, 0)
-    start_faces(0)
     build_spread()
     build_k()
     along_k()
     load_metric.wait()
     inside_rates(first)
-    await_all(0)
-    outside_rates(first, 0, finish_first)
-
+    await_chain(0)
+    chain_rates(first, 0)
+    await_faces(0)
+    face_rates(first, 0, finish_first)
+
+    pack_face(second, 1)
+    start_faces(1)
     pack(second, 1)
     start_chain(1)
-    pack_face(second, 1)
-    start_faces(1)
     along_k()
     inside_rates(second)
-    await_all(1)
-    outside_rates(second, 1, finish_second)
+    await_chain(1)
+    chain_rates(second, 1)
+    await_faces(1)
+    face_rates(second, 1, finish_second)
 
 
 def on_device(state, metric, block_map, links):

time: 16.6 us -> 16.5 us (level)
  no operation moved by 1% of the time
where the time goes in v2:
time: 16.5 us; the launch traced here: 16.3 us
  Pallas kernels  15.4 us (93%)
  local copies, waits for them, and re-layouts  0.82 us (5%)
    pallas_call x1, Pallas kernels, on_device(): pl.pallas_call(functools.partial(kernel, segs, chain, cross), out_shape=p...  15.4 us
    unnamed x1, local copies, waits for them, and re-layouts  0.82 us

profile of v2, /device:TPU:0, one launch (start us, length us, event | category | flops | bytes accessed | tf_op | source)
XLA Modules:
  0.0 16.3 jit_solution(7100730247212670945)
XLA Ops:
  0.0 15.4 %shard_map.46 = f32[4,16,2304]{2,1,0:T(8,128)S(1)} custom-call(f32[1,4,16,2304]{3,2,1,0:T(8,128)} %state_hbm.1, f32[1,9,16,2304]{3,2,1,0:T(8,128)} %metric_hbm.1, s32[32]{0:T(128)} %block_map.1, s32[6,4,32]{2,1,0:T(4,128)} %bitcast.3), custom_call_target="tpu_custom_call" | custom-call | tf_op jit(solution)/shard_map/pallas_call | solution.py:414
  15.4 0.8 %copy.6 = f32[1,4,16,2304]{3,2,1,0:T(8,128)} copy(f32[1,4,16,2304]{3,2,1,0:T(8,128)S(1)} %bitcast.2) | data formatting | bytes 1179648

commit v3 on v2

--- a/solution.py
+++ b/solution.py
@@ -113,14 +113,18 @@
         face_out[turn] = packed[:rows] + packed[rows:]
 
     def build_k():
-        for matrix in (k_slope_uvw, k_slope_p, k_bend):
-            matrix[...] = jnp.zeros((2 * chunk, chunk), jnp.bfloat16)
         low, high = own_layers[2], own_layers[3]
         here = lax.broadcasted_iota(jnp.int32, (cross, LANES), 0)
         column = lax.broadcasted_iota(jnp.int32, (cross, LANES), 1)
         for group in range(chunk // cross):
             first_row = group * cross
-            for tile in range(first_row // LANES, (first_row + cross - 1) // LANES + 1):
+            for tile in range(chunk // LANES):
+                lanes = slice(tile * LANES, (tile + 1) * LANES)
+                if not first_row // LANES <= tile <= (first_row + cross - 1) // LANES:
+                    for matrix in (k_slope_uvw, k_slope_p, k_bend):
+                        for top in (first_row, chunk + first_row):
+                            matrix[top:top + cross, lanes] = jnp.zeros((cross, LANES), jnp.bfloat16)
+                    continue
                 there = column + (tile * LANES - first_row)
                 there = jnp.where(jnp.logical_and(there >= 0, there < cross), there, 4 * width)
                 offset, mirrored = here - there, here + there
@@ -136,7 +140,6 @@
                               + at(mirrored, end, 8.0 * high) + at(mirrored, end - 1, -high))
                 wall_bend = (at(mirrored, 0, 16.0 * low) + at(mirrored, 1, -low)
                              + at(mirrored, end, 16.0 * high) + at(mirrored, end - 1, -high))
-                lanes = slice(tile * LANES, (tile + 1) * LANES)
                 for matrix, value in ((k_slope_uvw, slope + WALL[0] * wall_slope),
                                       (k_slope_p, slope + WALL[3] * wall_slope),
                                       (k_bend, bend + WALL[0] * wall_bend)):
@@ -376,6 +379,8 @@
         base = first[c, :, pl.ds(pl.multiple_of(start + LANES, LANES), chunk)]
         out_ref[c, :, pl.ds(start, chunk)] = 0.5 * base + 0.5 * (value + (time_step / 12.0) * rate)
 
+    build_spread()
+    build_k()
     load_state.wait()
     pack_face(first, 0)
     pl.semaphore_wait(barrier, segs - 1 + has_before.astype(jnp.int32) + has_after.astype(jnp.int32))
@@ -383,8 +388,6 @@
     start_faces(0)
     pack(first, 0)
     start_chain(0)
-    build_spread()
-    build_k()
     along_k()
     load_metric.wait()
     inside_rates(first)

time: 16.5 us -> 16.5 us (level)
  no operation moved by 1% of the time
where the time goes in v3:
time: 16.5 us; the launch traced here: 16.3 us
  Pallas kernels  15.4 us (93%)
  local copies, waits for them, and re-layouts  0.82 us (5%)
    pallas_call x1, Pallas kernels, on_device(): pl.pallas_call(functools.partial(kernel, segs, chain, cross), out_shape=p...  15.4 us
    unnamed x1, local copies, waits for them, and re-layouts  0.82 us

profile of v3, /device:TPU:0, one launch (start us, length us, event | category | flops | bytes accessed | tf_op | source)
XLA Modules:
  0.0 16.3 jit_solution(2317948554264798960)
XLA Ops:
  0.0 15.4 %shard_map.46 = f32[4,16,2304]{2,1,0:T(8,128)S(1)} custom-call(f32[1,4,16,2304]{3,2,1,0:T(8,128)} %state_hbm.1, f32[1,9,16,2304]{3,2,1,0:T(8,128)} %metric_hbm.1, s32[32]{0:T(128)} %block_map.1, s32[6,4,32]{2,1,0:T(4,128)} %bitcast.3), custom_call_target="tpu_custom_call" | custom-call | tf_op jit(solution)/shard_map/pallas_call | solution.py:417
  15.4 0.8 %copy.6 = f32[1,4,16,2304]{3,2,1,0:T(8,128)} copy(f32[1,4,16,2304]{3,2,1,0:T(8,128)S(1)} %bitcast.2) | data formatting | bytes 1179648
